TPU v7x, 32 devices: a whole 2x2x4 slice. The times are simulated.
32 devices in a mesh: batch: 4 (over x, core), blk: 8 (over z, y).
Axes of the slice: x: 2, y: 2, z: 4, core: 2. Of those that a mesh axis runs over, the one named last changes fastest.
Arguments:
- inputs: bfloat16 [32, 1024, 768], P('batch', 'blk'), may hold values from -6 to 6
- cotangent: bfloat16 [32, 1024, 768], P('batch', 'blk'), may hold values from -6 to 6
- group_counts: int32 [4], replicated, may hold values from 1 to 8, as said below
- first_gain: float32 [768], replicated, may hold values from 0.5 to 1.5
- first_bias: float32 [768], replicated, may hold values from -1.25 to 1.25
- qkv_weight: bfloat16 [768, 2304], replicated, may hold values from -0.21875 to 0.21875
- qkv_bias: float32 [2304], replicated, may hold values from -1.25 to 1.25
- out_weight: bfloat16 [768, 768], replicated, may hold values from -1.75 to 1.75
- out_bias: float32 [768], replicated, may hold values from -1.25 to 1.25
- second_gain: float32 [768], replicated, may hold values from 0.5 to 1.5
- second_bias: float32 [768], replicated, may hold values from -1.25 to 1.25
- up_weight: bfloat16 [768, 3072], replicated, may hold values from -0.21875 to 0.21875
- up_bias: float32 [3072], replicated, may hold values from -1.25 to 1.25
- down_weight: bfloat16 [3072, 768], replicated, may hold values from -0.109375 to 0.109375
- down_bias: float32 [768], replicated, may hold values from -1.25 to 1.25
- compress: bfloat16 [256, 1024], P(None, 'blk'), may hold values from -0.1875 to 0.1875
Outputs:
- output: bfloat16 [32, 1024, 768], P('batch', 'blk')
- input_grad: bfloat16 [32, 1024, 768], P('batch', 'blk')
- first_gain_grad: float32 [768], P('blk')
- first_bias_grad: float32 [768], P('blk')
- qkv_weight_grad: float32 [768, 2304], P('blk')
- qkv_bias_grad: float32 [2304], P('blk')
- out_weight_grad: float32 [768, 768], P('blk')
- out_bias_grad: float32 [768], P('blk')
- second_gain_grad: float32 [768], P('blk')
- second_bias_grad: float32 [768], P('blk')
- up_weight_grad: float32 [768, 3072], P('blk')
- up_bias_grad: float32 [3072], P('blk')
- down_weight_grad: float32 [3072, 768], P('blk')
- down_bias_grad: float32 [768], P('blk')
- compress_grad: float32 [256, 1024], P(None, 'blk')
Inputs may be any that keep to these rules, and one draw needn't show every extreme that they name: Group g holds sequences in its slots 0 to group_counts[g] - 1; the counts of all groups add up to exactly 20; in every draw some group uses all 8 slots and some group uses one.
All inputs are finite; a program needn't handle non-finite values.
Results may differ from a plain program's by a relative error of at most 0.02.
Values may be sent and summed in bfloat16 or wider, within the bound.
A program may use at most 192 MiB of HBM per device.

v0:
```python
import math

import jax
import jax.numpy as jnp
from jax import lax
from jax.sharding import PartitionSpec as P

H = 12
HD = 64


def layer_norm(states, factor, offset):
    center = states - jnp.mean(states, axis=-1, keepdims=True)
    spread = jnp.mean(center * center, axis=-1, keepdims=True)
    return center * lax.rsqrt(spread + 1e-05) * factor + offset


def gelu_tanh(values):
    return jax.nn.gelu(values, approximate=True)


def run_layer(
    inputs,
    cotangent,
    alive,
    first_gain,
    first_bias,
    qkv_weight,
    qkv_bias,
    out_weight,
    out_bias,
    second_gain,
    second_bias,
    up_weight,
    up_bias,
    down_weight,
    down_bias,
    compress,
):
    slots, tokens, width = inputs.shape
    rows = slots * tokens
    summary_len = compress.shape[0]
    factor = 1.0 / math.sqrt(HD)
    states = inputs.astype(jnp.float32)
    normed_first, first_back = jax.vjp(layer_norm, states, first_gain, first_bias)
    first_low = normed_first.astype(jnp.bfloat16).reshape(rows, width)
    project = jnp.dot(first_low, qkv_weight, preferred_element_type=jnp.float32) + qkv_bias
    query_low = project[:, :width].astype(jnp.bfloat16).reshape(slots, tokens, H, HD)
    pair_low = project[:, width:].astype(jnp.bfloat16).reshape(slots, tokens, 2 * width)
    partial_summary = jnp.einsum(
        "jt,stc->sjc", compress, pair_low, preferred_element_type=jnp.float32
    )
    summary_low = lax.psum(partial_summary, "blk").astype(jnp.bfloat16)
    key_low = summary_low[..., :width].reshape(slots, summary_len, H, HD)
    value_low = summary_low[..., width:].reshape(slots, summary_len, H, HD)
    scores = (
        jnp.einsum("sthd,sjhd->shtj", query_low, key_low, preferred_element_type=jnp.float32)
        * factor
    )
    highest = jnp.max(scores, axis=-1, keepdims=True)
    expo = jnp.exp(scores - highest)
    totals = jnp.sum(expo, axis=-1, keepdims=True)
    logsum = highest + jnp.log(totals)
    weights_low = (expo / totals).astype(jnp.bfloat16)
    mixed = jnp.einsum(
        "shtj,sjhd->sthd", weights_low, value_low, preferred_element_type=jnp.float32
    )
    mixed_low = mixed.reshape(rows, width).astype(jnp.bfloat16)
    branch = jnp.dot(mixed_low, out_weight, preferred_element_type=jnp.float32) + out_bias
    middle = states + branch.reshape(slots, tokens, width)
    second_normed, second_back = jax.vjp(layer_norm, middle, second_gain, second_bias)
    second_low = second_normed.astype(jnp.bfloat16).reshape(rows, width)
    hidden = jnp.dot(second_low, up_weight, preferred_element_type=jnp.float32) + up_bias
    active, gelu_back = jax.vjp(gelu_tanh, hidden)
    active_low = active.astype(jnp.bfloat16)
    result = middle + (
        jnp.dot(active_low, down_weight, preferred_element_type=jnp.float32) + down_bias
    ).reshape(slots, tokens, width)
    output = jnp.where(alive, result, 0.0).astype(jnp.bfloat16)
    incoming = jnp.where(alive, cotangent, jnp.zeros_like(cotangent)).reshape(rows, width)
    incoming_full = incoming.astype(jnp.float32)
    down_grad = jnp.einsum("rf,rd->fd", active_low, incoming, preferred_element_type=jnp.float32)
    down_bias_grad = jnp.sum(incoming_full, axis=0)
    active_grad = jnp.einsum("rd,fd->rf", incoming, down_weight, preferred_element_type=jnp.float32)
    hidden_low = gelu_back(active_grad)[0].astype(jnp.bfloat16)
    up_grad = jnp.einsum("rd,rf->df", second_low, hidden_low, preferred_element_type=jnp.float32)
    up_bias_grad = jnp.sum(hidden_low.astype(jnp.float32), axis=0)
    second_grad = jnp.einsum("rf,df->rd", hidden_low, up_weight, preferred_element_type=jnp.float32)
    middle_part, second_gain_grad, second_bias_grad = second_back(
        second_grad.reshape(slots, tokens, width)
    )
    middle_grad = incoming_full.reshape(slots, tokens, width) + middle_part
    branch_low = middle_grad.reshape(rows, width).astype(jnp.bfloat16)
    out_grad = jnp.einsum("rd,re->de", mixed_low, branch_low, preferred_element_type=jnp.float32)
    out_bias_grad = jnp.sum(branch_low.astype(jnp.float32), axis=0)
    mixed_grad = jnp.einsum("re,de->rd", branch_low, out_weight, preferred_element_type=jnp.float32)
    mixed_grad_low = mixed_grad.astype(jnp.bfloat16).reshape(slots, tokens, H, HD)
    scores_again = (
        jnp.einsum("sthd,sjhd->shtj", query_low, key_low, preferred_element_type=jnp.float32)
        * factor
    )
    weights_again = jnp.exp(scores_again - logsum)
    weights_again_low = weights_again.astype(jnp.bfloat16)
    weight_grad = jnp.einsum(
        "sthd,sjhd->shtj", mixed_grad_low, value_low, preferred_element_type=jnp.float32
    )
    value_summary_grad = jnp.einsum(
        "shtj,sthd->sjhd", weights_again_low, mixed_grad_low, preferred_element_type=jnp.float32
    )
    inner = jnp.sum(weights_again * weight_grad, axis=-1, keepdims=True)
    score_low = (weights_again * (weight_grad - inner)).astype(jnp.bfloat16)
    query_grad = (
        jnp.einsum("shtj,sjhd->sthd", score_low, key_low, preferred_element_type=jnp.float32)
        * factor
    )
    key_summary_grad = (
        jnp.einsum("shtj,sthd->sjhd", score_low, query_low, preferred_element_type=jnp.float32)
        * factor
    )
    summary_grad = jnp.concatenate(
        [
            key_summary_grad.reshape(slots, summary_len, width),
            value_summary_grad.reshape(slots, summary_len, width),
        ],
        axis=-1,
    )
    summary_grad_low = lax.psum(summary_grad.astype(jnp.bfloat16), "blk")
    pair_grad = jnp.einsum(
        "jt,sjc->stc", compress, summary_grad_low, preferred_element_type=jnp.float32
    )
    compress_grad = jnp.einsum(
        "sjc,stc->jt", summary_grad_low, pair_low, preferred_element_type=jnp.float32
    )
    project_low = jnp.concatenate(
        [query_grad.reshape(rows, width), pair_grad.reshape(rows, 2 * width)], axis=-1
    ).astype(jnp.bfloat16)
    qkv_grad = jnp.einsum("rd,rc->dc", first_low, project_low, preferred_element_type=jnp.float32)
    qkv_bias_grad = jnp.sum(project_low.astype(jnp.float32), axis=0)
    first_grad = jnp.einsum(
        "rc,dc->rd", project_low, qkv_weight, preferred_element_type=jnp.float32
    )
    state_part, first_gain_grad, first_bias_grad = first_back(
        first_grad.reshape(slots, tokens, width)
    )
    input_grad = (middle_grad + state_part).astype(jnp.bfloat16)
    grads = (
        first_gain_grad,
        first_bias_grad,
        qkv_grad,
        qkv_bias_grad,
        out_grad,
        out_bias_grad,
        second_gain_grad,
        second_bias_grad,
        up_grad,
        up_bias_grad,
        down_grad,
        down_bias_grad,
    )
    return (output, input_grad, grads, compress_grad)


def body(
    inputs,
    cotangent,
    group_counts,
    first_gain,
    first_bias,
    qkv_weight,
    qkv_bias,
    out_weight,
    out_bias,
    second_gain,
    second_bias,
    up_weight,
    up_bias,
    down_weight,
    down_bias,
    compress,
):
    slots = inputs.shape[0]
    weights_all = (
        first_gain,
        first_bias,
        qkv_weight,
        qkv_bias,
        out_weight,
        out_bias,
        second_gain,
        second_bias,
        up_weight,
        up_bias,
        down_weight,
        down_bias,
        compress,
    )
    group_index = lax.axis_index("batch")
    my_count = group_counts[group_index]
    alive = (jnp.arange(slots, dtype=jnp.int32) < my_count)[:, None, None]
    output, input_grad, grads, compress_grad = run_layer(inputs, cotangent, alive, *weights_all)
    (
        first_gain_grad,
        first_bias_grad,
        qkv_grad,
        qkv_bias_grad,
        out_grad,
        out_bias_grad,
        second_gain_grad,
        second_bias_grad,
        up_grad,
        up_bias_grad,
        down_grad,
        down_bias_grad,
    ) = grads
    (
        first_gain_rows,
        first_bias_rows,
        qkv_rows,
        qkv_bias_rows,
        out_rows,
        out_bias_rows,
        second_gain_rows,
        second_bias_rows,
        up_rows,
        up_bias_rows,
        down_rows,
        down_bias_rows,
    ) = (
        lax.psum_scatter(
            first_gain_grad.astype(jnp.bfloat16), "blk", scatter_dimension=0, tiled=True
        ).astype(jnp.float32),
        lax.psum_scatter(
            first_bias_grad.astype(jnp.bfloat16), "blk", scatter_dimension=0, tiled=True
        ).astype(jnp.float32),
        lax.psum_scatter(
            qkv_grad.astype(jnp.bfloat16), "blk", scatter_dimension=0, tiled=True
        ).astype(jnp.float32),
        lax.psum_scatter(
            qkv_bias_grad.astype(jnp.bfloat16), "blk", scatter_dimension=0, tiled=True
        ).astype(jnp.float32),
        lax.psum_scatter(
            out_grad.astype(jnp.bfloat16), "blk", scatter_dimension=0, tiled=True
        ).astype(jnp.float32),
        lax.psum_scatter(
            out_bias_grad.astype(jnp.bfloat16), "blk", scatter_dimension=0, tiled=True
        ).astype(jnp.float32),
        lax.psum_scatter(
            second_gain_grad.astype(jnp.bfloat16), "blk", scatter_dimension=0, tiled=True
        ).astype(jnp.float32),
        lax.psum_scatter(
            second_bias_grad.astype(jnp.bfloat16), "blk", scatter_dimension=0, tiled=True
        ).astype(jnp.float32),
        lax.psum_scatter(
            up_grad.astype(jnp.bfloat16), "blk", scatter_dimension=0, tiled=True
        ).astype(jnp.float32),
        lax.psum_scatter(
            up_bias_grad.astype(jnp.bfloat16), "blk", scatter_dimension=0, tiled=True
        ).astype(jnp.float32),
        lax.psum_scatter(
            down_grad.astype(jnp.bfloat16), "blk", scatter_dimension=0, tiled=True
        ).astype(jnp.float32),
        lax.psum_scatter(
            down_bias_grad.astype(jnp.bfloat16), "blk", scatter_dimension=0, tiled=True
        ).astype(jnp.float32),
    )
    summed = (
        lax.psum(first_gain_rows.astype(jnp.bfloat16), "batch").astype(jnp.float32),
        lax.psum(first_bias_rows.astype(jnp.bfloat16), "batch").astype(jnp.float32),
        lax.psum(qkv_rows.astype(jnp.bfloat16), "batch").astype(jnp.float32),
        lax.psum(qkv_bias_rows.astype(jnp.bfloat16), "batch").astype(jnp.float32),
        lax.psum(out_rows.astype(jnp.bfloat16), "batch").astype(jnp.float32),
        lax.psum(out_bias_rows.astype(jnp.bfloat16), "batch").astype(jnp.float32),
        lax.psum(second_gain_rows.astype(jnp.bfloat16), "batch").astype(jnp.float32),
        lax.psum(second_bias_rows.astype(jnp.bfloat16), "batch").astype(jnp.float32),
        lax.psum(up_rows.astype(jnp.bfloat16), "batch").astype(jnp.float32),
        lax.psum(up_bias_rows.astype(jnp.bfloat16), "batch").astype(jnp.float32),
        lax.psum(down_rows.astype(jnp.bfloat16), "batch").astype(jnp.float32),
        lax.psum(down_bias_rows.astype(jnp.bfloat16), "batch").astype(jnp.float32),
        lax.psum(compress_grad.astype(jnp.bfloat16), "batch").astype(jnp.float32),
    )
    return (output, input_grad) + tuple(summed)


def solution(mesh):
    placed = (
        P("batch", "blk", None),
        P("batch", "blk", None),
        P(),
        P(),
        P(),
        P(),
        P(),
        P(),
        P(),
        P(),
        P(),
        P(),
        P(),
        P(),
        P(),
        P(None, "blk"),
    )
    return jax.shard_map(
        body,
        mesh=mesh,
        in_specs=placed,
        out_specs=(
            P("batch", "blk", None),
            P("batch", "blk", None),
            P("blk"),
            P("blk"),
            P("blk", None),
            P("blk"),
            P("blk", None),
            P("blk"),
            P("blk"),
            P("blk"),
            P("blk", None),
            P("blk"),
            P("blk", None),
            P("blk"),
            P(None, "blk"),
        ),
        check_vma=False,
    )
```

profile of v0, /device:TPU:1, one launch (start us, length us, event | category | flops | bytes accessed | tf_op | source)
XLA Modules:
  0.0 1305.9 jit_solution(606664537931861903)
XLA Ops:
  26.8 7.2 convolution_bitcast_fusion
  34.0 486.1 %all-reduce.18 = bf16[8,256,1536]{1,2,0:T(8,128)(2,1)} all-reduce(f32[8,256,1536]{1,2,0:T(8,128)} %convolution_bitcast_fusion), channel_id=1, replica_groups=mesh['batch'=4,'blk'=8] {'blk'}, use_global_device_ids=true, to_apply=%region_2.0 | all-reduce | flops 3145728 | bytes 18874368 | tf_op jit(solution)/shard_map/psum | solution.py:53
  531.1 6.3 fusion.36
  545.5 8.0 fusion.66
  553.5 11.1 convolution_add_fusion.1
  564.6 16.9 %fusion.65 = (bf16[3072]{0:T(1024)(128)(2,1)}, bf16[1024,3072]{1,0:T(8,128)(2,1)}) fusion(f32[1024,3072]{1,0:T(8,128)} %fusion.66, f32[3072]{0:T(1024)S(1)} %copy-done.40, bf16[1024,768]{1,0:T(8,128)(2,1)S(1)} %bitcast.116, bf16[3072,768]{1,0:T(8,128)(2,1)S(1)} %bitcast.135), kind=kOutput, calls=%fused_computation.106 | convolution fusion | flops 4901041152 | bytes 25184256 | tf_op jit(solution)/shard_map/rd,fd->rf/dot_general | solution.py:84
  581.5 9.2 fusion.64
  609.4 7.3 fusion.25
  616.7 13.5 %multiply_reduce_fusion = (f32[8,12,128]{2,1,0:T(8,128)}, f32[8,12,128,256]{3,2,1,0:T(8,128)}) fusion(f32[8,12,128,256]{3,2,1,0:T(8,128)} %copy-done.1, f32[8,12,128]{2,1,0:T(8,128)S(1)} %copy-done.23, bf16[8,256,12,64]{1,3,2,0:T(8,128)(2,1)S(1)} %bitcast.119, bf16[8,128,12,64]{1,0,3,2:T(8,128)(2,1)S(1)} %bitcast.112), kind=kOutput, calls=%fused_computation.10 | convolution fusion | flops 415223808 | bytes 29982720 | tf_op jit(solution)/shard_map/sthd,sjhd->shtj/dot_general | solution.py:104
  634.8 10.4 multiply_convert_fusion
  653.5 6.0 pad_maximum_fusion
  663.9 12.9 convolution_convert_fusion
  676.9 9.2 convolution_convert_fusion.1
  686.2 6.1 fusion.37
  698.0 171.9 %all-reduce.15.cloned.1.call-done = bf16[8,256,1536]{2,1,0:T(8,128)(2,1)} async-done(((bf16[8,256,1536]{2,1,0:T(8,128)(2,1)}), bf16[8,256,1536]{2,1,0:T(8,128)(2,1)}) %all-reduce.15.cloned.1.call-update) | async-done | bytes 6291472 | tf_op jit(solution)/shard_map/psum | solution.py:127
  875.6 5.4 convolution_convert_fusion.2
  884.1 6.4 fusion.63
  897.9 37.8 %reduce-scatter.7.cloned.1.call-done = bf16[96,768]{1,0:T(8,128)(2,1)} async-done(((bf16[768,768]{1,0:T(8,128)(2,1)}), bf16[96,768]{1,0:T(8,128)(2,1)}) %reduce-scatter.7.cloned.1.call-update) | async-done | bytes 147472 | tf_op jit(solution)/shard_map/reduce_scatter | solution.py:241
  935.7 99.9 %reduce-scatter.11.cloned.1.call-done = bf16[384,768]{1,0:T(8,128)(2,1)} async-done(((bf16[3072,768]{1,0:T(8,128)(2,1)}), bf16[384,768]{1,0:T(8,128)(2,1)}) %reduce-scatter.11.cloned.1.call-update) | async-done | bytes 589840 | tf_op jit(solution)/shard_map/reduce_scatter | solution.py:259
  1035.6 99.0 %reduce-scatter.9.cloned.1.call-done = bf16[96,3072]{1,0:T(8,128)(2,1)} async-done(((bf16[768,3072]{1,0:T(8,128)(2,1)}), bf16[96,3072]{1,0:T(8,128)(2,1)}) %reduce-scatter.9.cloned.1.call-update) | async-done | bytes 589840 | tf_op jit(solution)/shard_map/reduce_scatter | solution.py:253
  1134.6 82.7 %reduce-scatter.5.cloned.1.call-done = bf16[96,2304]{1,0:T(8,128)(2,1)} async-done(((bf16[768,2304]{1,0:T(8,128)(2,1)}), bf16[96,2304]{1,0:T(8,128)(2,1)}) %reduce-scatter.5.cloned.1.call-update) | async-done | bytes 442384 | tf_op jit(solution)/shard_map/reduce_scatter | solution.py:235
  1220.9 29.7 %all-reduce.8 = (bf16[768]{0:T(1024)(128)(2,1)}, bf16[768]{0:T(1024)(128)(2,1)}, bf16[2304]{0:T(1024)(128)(2,1)}, bf16[768]{0:T(1024)(128)(2,1)}, bf16[768]{0:T(...) all-reduce(bf16[768]{0:T(1024)(128)(2,1)} %get-tuple-element.17, ...), channel_id=2, replica_groups=mesh['batch'=4,'blk'=8] {'blk'}, use_global_device_ids=true, to_apply=%region_14.15.clone | all-reduce | flops 9984 | bytes 39936
  1260.8 14.1 %all-reduce.9 = (bf16[96]{0:T(256)(128)(2,1)}, bf16[96]{0:T(256)(128)(2,1)}, bf16[288]{0:T(512)(128)(2,1)}, bf16[96]{0:T(256)(128)(2,1)}, bf16[96]{0:T(256)(128)...) all-reduce(bf16[96]{0:T(256)(128)(2,1)} %dynamic-slice.1, ...), channel_id=1, replica_groups=mesh['batch'=4,'blk'=8] {'batch'}, use_global_device_ids=true, to_apply=%region_15.16 | all-reduce | flops 1248 | bytes 4992 | tf_op jit(solution)/shard_map/psum | solution.py:267
  1285.0 5.4 add_convert_fusion.1
  (187 shorter events, 126.8 us)
Async XLA Ops:
  7.2 5.4 copy-start
  7.2 862.7 %all-reduce.15.cloned.1.call-start = ((), (), s32[]{:S(2)}) async-start(), calls=%async_computation.4 | async-start | bytes 12582912 | tf_op jit(solution)/shard_map/psum | solution.py:127
  7.3 5.3 copy-start.39
  523.6 7.5 copy-start.14
  526.3 4.8 copy-start.1
  543.7 20.9 %copy-start.13 = (bf16[8,128,768]{2,1,0:T(8,128)(2,1)}, bf16[8,128,768]{2,1,0:T(8,128)(2,1)S(1)}, u32[]{:S(2)}) copy-start(bf16[8,128,768]{2,1,0:T(8,128)(2,1)S(1)} %get-tuple-element.41) | copy-start | bytes 4718596
  543.7 9.7 slice-start.2
  545.4 8.0 slice-start.3
  545.5 8.0 copy-start.40
  545.5 8.0 copy-start.42
  597.6 4.8 copy-start.38
  609.4 7.3 copy-start.15
  634.8 10.4 copy-start.12
  659.5 276.2 %reduce-scatter.7.cloned.1.call-start = ((), (), s32[]{:S(2)}) async-start(), calls=%async_computation.6 | async-start | bytes 1327104 | tf_op jit(solution)/shard_map/reduce_scatter | solution.py:241
  663.9 371.7 %reduce-scatter.11.cloned.1.call-start = ((), (), s32[]{:S(2)}) async-start(), calls=%async_computation.8 | async-start | bytes 5308416 | tf_op jit(solution)/shard_map/reduce_scatter | solution.py:259
  676.9 457.7 %reduce-scatter.9.cloned.1.call-start = ((), (), s32[]{:S(2)}) async-start(), calls=%async_computation.7 | async-start | bytes 5308416 | tf_op jit(solution)/shard_map/reduce_scatter | solution.py:253
  686.1 531.1 %reduce-scatter.5.cloned.1.call-start = ((), (), s32[]{:S(2)}) async-start(), calls=%async_computation.5 | async-start | bytes 3981312 | tf_op jit(solution)/shard_map/reduce_scatter | solution.py:235
  869.9 5.7 copy-start.16
  869.9 5.7 copy-start.19
  880.9 409.5 %all-reduce.17.cloned.1.call-start = ((), (), s32[]{:S(2)}) async-start(), calls=%async_computation.9 | async-start | bytes 3670016 | tf_op jit(solution)/shard_map/psum | solution.py:269
  884.1 6.5 copy-start.4
  884.1 6.5 copy-start.26
  884.1 6.5 copy-start.30
  1290.4 7.4 copy-start.24
  (33 other events, 82.9 us)
Sparse Core Ops, SparseCore 0:
  659.7 210.1 all-reduce.14
  874.2 61.4 reduce-scatter.6
  939.8 95.7 reduce-scatter.10
  1039.5 94.9 reduce-scatter.8
  1138.5 78.7 reduce-scatter.4
  1220.6 47.3 all-reduce.16
where the time goes:
time: 1310 us
  blocking collectives  530 us (40%)
  waiting for transfers between devices  491 us (37%)
  matrix products  144 us (11%)
  other arithmetic  70.1 us (5%)
  local copies, waits for them, and re-layouts  53.4 us (4%)
  between operations  17 us (1%)
    psum x1, blocking collectives, run_layer(): summary_low = lax.psum(partial_summary, 'blk').astype(jnp.bfloat16)  486 us
    psum x1, waiting for transfers between devices, run_layer(): summary_grad_low = lax.psum(summary_grad.astype(jnp.bfloat16), 'blk')  172 us
    reduce_scatter x1, waiting for transfers between devices, body(): lax.psum_scatter(down_grad.astype(jnp.bfloat16), 'blk', scatter_dimension...  99.9 us
    reduce_scatter x1, waiting for transfers between devices, body(): lax.psum_scatter(up_grad.astype(jnp.bfloat16), 'blk', scatter_dimension=0...  99 us
    reduce_scatter x1, waiting for transfers between devices, body(): lax.psum_scatter(qkv_grad.astype(jnp.bfloat16), 'blk', scatter_dimension=...  82.7 us
    reduce_scatter x1, waiting for transfers between devices, body(): lax.psum_scatter(out_grad.astype(jnp.bfloat16), 'blk', scatter_dimension=...  37.8 us
    unnamed x1, blocking collectives  29.7 us
    unnamed x114, local copies, waits for them, and re-layouts  26.4 us
  transfers between devices with their start and end apart: 6, of which 5 were waited for; matrix products, arithmetic and copies ran while one was open for 7% of the time, Pallas kernels for 0%

commit v1 on v0

v1 whole, which is shorter than its diff:
```python
import functools
import math

import jax
import jax.numpy as jnp
from jax import lax
from jax.sharding import PartitionSpec as P

H = 12
HD = 64
F32 = jnp.float32
BF16 = jnp.bfloat16


def norm_stats(states):
    center = states - jnp.mean(states, axis=-1, keepdims=True)
    spread = jnp.mean(center * center, axis=-1, keepdims=True)
    rate = lax.rsqrt(spread + 1e-05)
    return center * rate, rate


def norm_back(hat, rate, upstream, gain):
    scaled = upstream * gain
    return rate * (
        scaled
        - jnp.mean(scaled, axis=-1, keepdims=True)
        - hat * jnp.mean(scaled * hat, axis=-1, keepdims=True)
    )


def dot(a, b):
    return jnp.dot(a, b, preferred_element_type=F32)


def dot_t(a, b):
    return lax.dot_general(a, b, (((1,), (1,)), ((), ())), preferred_element_type=F32)


def t_dot(a, b):
    return lax.dot_general(a, b, (((0,), (0,)), ((), ())), preferred_element_type=F32)


def swap(values, axis, size, bit):
    return lax.ppermute(values, axis, [(i, i ^ bit) for i in range(size)])


def halve(values, dim, axis, size, bit):
    mine = (lax.axis_index(axis) // bit) % 2
    send = lax.dynamic_index_in_dim(values, 1 - mine, dim, keepdims=False).astype(BF16)
    keep = lax.dynamic_index_in_dim(values, mine, dim, keepdims=False)
    return keep.astype(F32) + swap(send, axis, size, bit).astype(F32)


def scatter_sum(terms, bits, order, nb, nk):
    _, rows, cols = terms.shape
    values = halve(terms.reshape(-1, 2, rows // 2, cols), 1, "batch", nb, 1)
    left = list(bits)
    for bit in order:
        place = left.index(bit)
        values = values.reshape(1 << place, 2, -1, rows // 2, cols)
        values = halve(values, 1, "blk", nk, bit)
        left.remove(bit)
    values = values.reshape(rows // 2, cols)
    bit = 2
    while bit < nb:
        low = values.astype(BF16)
        values = low.astype(F32) + swap(low, "batch", nb, bit).astype(F32)
        bit *= 2
    mine = lax.axis_index("batch") % 2
    other = swap(values, "batch", nb, 1)
    first = jnp.where(mine == 0, values, other)
    second = jnp.where(mine == 0, other, values)
    return jnp.concatenate([first, second], axis=0)


def body(
    inputs,
    cotangent,
    group_counts,
    first_gain,
    first_bias,
    qkv_weight,
    qkv_bias,
    out_weight,
    out_bias,
    second_gain,
    second_bias,
    up_weight,
    up_bias,
    down_weight,
    down_bias,
    compress,
    *,
    nb,
    nk,
):
    slots, tokens, width = inputs.shape
    splits = nk // slots
    teams = [[t * slots + i for i in range(slots)] for t in range(splits)]
    across = [[t * slots + i for t in range(splits)] for i in range(slots)]
    rows = slots * tokens

    def gather_rows(values):
        return lax.all_to_all(values, "blk", 0, 0, axis_index_groups=teams, tiled=True).reshape(
            rows, width
        )

    def spread_rows(values):
        return lax.all_to_all(
            values.reshape(slots, tokens, width), "blk", 0, 0, axis_index_groups=teams, tiled=True
        )

    def over_splits(values):
        if splits == 1:
            return values
        return lax.psum(values, "blk", axis_index_groups=across)

    slot = lax.axis_index("blk") % slots
    alive = slot < group_counts[lax.axis_index("batch")]

    low_x = gather_rows(inputs)
    squeeze = lax.all_gather(compress, "blk", axis=1, tiled=True, axis_index_groups=teams)
    low_cot = gather_rows(cotangent)
    incoming = jnp.where(alive, low_cot, jnp.zeros_like(low_cot))

    states = low_x.astype(F32)
    hat_first, rate_first = norm_stats(states)
    normed = (hat_first * first_gain + first_bias).astype(BF16)
    query_weight, pair_weight = qkv_weight[:, :width], qkv_weight[:, width:]
    query_bias, pair_bias = qkv_bias[:width], qkv_bias[width:]
    query = (dot(normed, query_weight) + query_bias).astype(BF16)
    core = over_splits(dot(squeeze, normed)).astype(BF16)
    total = over_splits(jnp.sum(squeeze.astype(F32), axis=1))
    pair = (dot(core, pair_weight) + total[:, None] * pair_bias).astype(BF16)

    factor = 1.0 / math.sqrt(HD)
    query_heads = query.reshape(rows, H, HD)
    key_heads = pair[:, :width].reshape(-1, H, HD)
    value_heads = pair[:, width:].reshape(-1, H, HD)
    scores = (
        jnp.einsum("thd,jhd->htj", query_heads, key_heads, preferred_element_type=F32) * factor
    )
    expo = jnp.exp(scores - jnp.max(scores, axis=-1, keepdims=True))
    weights = expo / jnp.sum(expo, axis=-1, keepdims=True)
    weights_low = weights.astype(BF16)
    mixed = (
        jnp.einsum("htj,jhd->thd", weights_low, value_heads, preferred_element_type=F32)
        .reshape(rows, width)
        .astype(BF16)
    )
    middle = states + dot(mixed, out_weight) + out_bias
    hat_second, rate_second = norm_stats(middle)
    second = (hat_second * second_gain + second_bias).astype(BF16)
    hidden = dot(second, up_weight) + up_bias
    active, gelu_back = jax.vjp(functools.partial(jax.nn.gelu, approximate=True), hidden)
    active_low = active.astype(BF16)
    result = middle + dot(active_low, down_weight) + down_bias
    output = spread_rows(jnp.where(alive, result, 0.0).astype(BF16))

    incoming_full = incoming.astype(F32)
    down_grad = t_dot(active_low, incoming)
    down_bias_grad = jnp.sum(incoming_full, axis=0)
    hidden_low = gelu_back(dot_t(incoming, down_weight))[0].astype(BF16)
    up_grad = t_dot(second, hidden_low)
    up_bias_grad = jnp.sum(hidden_low.astype(F32), axis=0)
    second_up = dot_t(hidden_low, up_weight)
    second_gain_grad = jnp.sum(second_up * hat_second, axis=0)
    second_bias_grad = jnp.sum(second_up, axis=0)
    middle_grad = incoming_full + norm_back(hat_second, rate_second, second_up, second_gain)
    branch_low = middle_grad.astype(BF16)
    out_grad = t_dot(mixed, branch_low)
    out_bias_grad = jnp.sum(branch_low.astype(F32), axis=0)
    mixed_grad = dot_t(branch_low, out_weight).astype(BF16).reshape(rows, H, HD)

    weight_grad = jnp.einsum("thd,jhd->htj", mixed_grad, value_heads, preferred_element_type=F32)
    inner = jnp.sum(weights * weight_grad, axis=-1, keepdims=True)
    score_low = (weights * (weight_grad - inner)).astype(BF16)
    value_back = jnp.einsum("htj,thd->jhd", weights_low, mixed_grad, preferred_element_type=F32)
    key_back = (
        jnp.einsum("htj,thd->jhd", score_low, query_heads, preferred_element_type=F32) * factor
    )
    query_back = (
        jnp.einsum("htj,jhd->thd", score_low, key_heads, preferred_element_type=F32) * factor
    )
    pair_back = jnp.concatenate(
        [key_back.reshape(-1, width), value_back.reshape(-1, width)], axis=1
    )
    pair_back_low = pair_back.astype(BF16)
    query_back_low = query_back.reshape(rows, width).astype(BF16)
    core_back = over_splits(dot_t(pair_back_low, pair_weight)).astype(BF16)
    lift = over_splits(jnp.sum(pair_back * pair_bias, axis=1))
    query_weight_grad = t_dot(normed, query_back_low)
    pair_weight_grad = t_dot(core, pair_back_low)
    qkv_grad = jnp.concatenate([query_weight_grad, pair_weight_grad], axis=1)
    qkv_bias_grad = jnp.concatenate(
        [
            jnp.sum(query_back_low.astype(F32), axis=0),
            jnp.sum(total[:, None] * pair_back, axis=0),
        ]
    )
    first_up = dot_t(query_back_low, query_weight) + t_dot(squeeze, core_back)
    first_gain_grad = jnp.sum(first_up * hat_first, axis=0)
    first_bias_grad = jnp.sum(first_up, axis=0)
    input_grad = spread_rows(
        (middle_grad + norm_back(hat_first, rate_first, first_up, first_gain)).astype(BF16)
    )
    compress_terms = (
        jnp.einsum(
            "jc,btc->bjt",
            core_back,
            normed.reshape(slots, tokens, width),
            preferred_element_type=F32,
        )
        + lift[None, :, None]
    )

    low_first = [1 << i for i in range(nk.bit_length() - 1)]
    high_first = low_first[::-1]
    team_low = [1 << i for i in range(slots.bit_length() - 1)]

    def matrix(grad):
        blocks = grad.reshape(nk, grad.shape[0] // nk, grad.shape[1])
        return scatter_sum(blocks, high_first, low_first, nb, nk)

    down_rows = matrix(down_grad)
    up_rows = matrix(up_grad)
    out_rows = matrix(out_grad)
    qkv_rows = matrix(qkv_grad)
    compress_rows = scatter_sum(compress_terms, team_low[::-1], team_low, nb, nk)
    vectors = (
        first_gain_grad,
        first_bias_grad,
        qkv_bias_grad,
        out_bias_grad,
        second_gain_grad,
        second_bias_grad,
        up_bias_grad,
        down_bias_grad,
    )
    packed = jnp.concatenate([v.reshape(nk, -1) for v in vectors], axis=1)
    packed = lax.psum(packed, ("batch", "blk"))
    mine = lax.dynamic_index_in_dim(packed, lax.axis_index("blk"), 0, keepdims=False)
    pieces = []
    start = 0
    for v in vectors:
        size = v.shape[0] // nk
        pieces.append(mine[start : start + size])
        start += size
    (fg, fb, qb, ob, sg, sb, ub, db) = pieces
    return (
        output,
        input_grad,
        fg,
        fb,
        qkv_rows,
        qb,
        out_rows,
        ob,
        sg,
        sb,
        up_rows,
        ub,
        down_rows,
        db,
        compress_rows,
    )


def solution(mesh):
    rows = P("batch", "blk", None)
    placed = (rows, rows) + (P(),) * 13 + (P(None, "blk"),)
    vec, mat = P("blk"), P("blk", None)
    return jax.shard_map(
        functools.partial(body, nb=mesh.shape["batch"], nk=mesh.shape["blk"]),
        mesh=mesh,
        in_specs=placed,
        out_specs=(rows, rows, vec, vec, mat, vec, mat, vec, vec, vec, mat, vec, mat, vec, P(None, "blk")),
        check_vma=False,
    )
```

time: 1310 us -> 491 us (0.37)
  blocking collectives: 530 us -> 94.2 us
  waiting for transfers between devices: 491 us -> 108 us
  starting transfers between devices: 0.25 us -> 62.9 us
  other arithmetic: 70.1 us -> 41.6 us
  matrix products: 144 us -> 118 us
  between operations: 17 us -> 3.14 us
    psum x2 -> x1, blocking collectives: 500 us -> 41.7 us  [body(): packed = lax.psum(packed, ('batch', 'blk'))]
    reduce_scatter x4 -> x0, waiting for transfers between devices: 319 us -> none  [the longest x1 99.9 us: body(): lax.psum_scatter(down_grad.astype(jnp.bfloat16), 'blk', scatter_dimension...]
    psum x2 -> x0, waiting for transfers between devices: 172 us -> none  [the longest x1 172 us: run_layer(): summary_grad_low = lax.psum(summary_grad.astype(jnp.bfloat16), 'blk')]
    ppermute x0 -> x30, waiting for transfers between devices: none -> 108 us  [swap(): return lax.ppermute(values, axis, [(i, i ^ bit) for i in range(size)])]
    all_gather x0 -> x1, blocking collectives: none -> 52.5 us  [body(): lax.all_gather(compress, 'blk', axis=1, tiled=True, axis_index_groups=teams)]
    ppermute x0 -> x30, starting transfers between devices: none -> 43.4 us  [swap(): return lax.ppermute(values, axis, [(i, i ^ bit) for i in range(size)])]
    dot_general x21 -> x23, matrix products: 144 us -> 108 us  [the longest x5 33 us: dot_t(): lax.dot_general(a, b, (((1,), (1,)), ((), ())), preferred_element_type=F32)]
    unnamed x1 -> x0, blocking collectives: 29.7 us -> none
  transfers between devices with their start and end apart: 6 -> 34, of which waited for: 5 -> 11; matrix products, arithmetic and copies ran while one was open for 7% -> 21% of each run, Pallas kernels for 0% -> 0%
where the time goes in v1:
time: 491 us; the launch traced here: 482 us
  matrix products  118 us (24%)
  waiting for transfers between devices  108 us (22%)
  blocking collectives  94.2 us (19%)
  starting transfers between devices  62.9 us (13%)
  local copies, waits for them, and re-layouts  53 us (11%)
  other arithmetic  41.6 us (8%)
    ppermute x30, waiting for transfers between devices, swap(): return lax.ppermute(values, axis, [(i, i ^ bit) for i in range(size)])  108 us
    all_gather x1, blocking collectives, body(): lax.all_gather(compress, 'blk', axis=1, tiled=True, axis_index_groups=teams)  52.5 us
    ppermute x30, starting transfers between devices, swap(): return lax.ppermute(values, axis, [(i, i ^ bit) for i in range(size)])  43.4 us
    psum x1, blocking collectives, body(): packed = lax.psum(packed, ('batch', 'blk'))  41.7 us
    dot_general x5, matrix products, dot_t(): lax.dot_general(a, b, (((1,), (1,)), ((), ())), preferred_element_type=F32)  33 us
    dot_general x6, matrix products, dot(): return jnp.dot(a, b, preferred_element_type=F32)  30.6 us
    dot_general x6, matrix products, t_dot(): lax.dot_general(a, b, (((0,), (0,)), ((), ())), preferred_element_type=F32)  23.9 us
    unnamed x155, local copies, waits for them, and re-layouts  19 us
  transfers between devices with their start and end apart: 34, of which 11 were waited for; matrix products, arithmetic and copies ran while one was open for 21% of the time, Pallas kernels for 0%

profile of v1, /device:TPU:1, one launch (start us, length us, event | category | flops | bytes accessed | tf_op | source)
XLA Modules:
  0.0 481.7 jit_solution(5319059662885818010)
XLA Ops:
  0.7 6.5 %all-to-all-start = ((bf16[8,128,768]{2,1,0:T(8,128)(2,1)}), bf16[8,128,768]{2,1,0:T(8,128)(2,1)S(1)}, u32[]{:S(2)}, u32[]{:S(2)}) async-start(bf16[8,128,768]{2,1,0:T(8,128)(2,1)} %param.16), calls=%async_computation | async-start | bytes 3145728 | tf_op jit(solution)/shard_map/all_to_all | solution.py:104
  8.6 52.5 %all_gather.3 = bf16[256,1024]{1,0:T(8,128)(2,1)S(1)} all-gather(bf16[256,128]{1,0:T(8,128)(2,1)S(1)} %copy-done.33), channel_id=1, replica_groups={{0,1,2,3,4,5,6,7},{8,9,10,11,12,13,14,15},{16,17,18,19,20,21,22,23},{24..., dimensions={1}, use_global_device_ids=true | all-gather | bytes 589824 | tf_op jit(solution)/shard_map/all_gather | solution.py:122
  75.5 10.7 %fusion.102 = (f32[12,1024]{1,0:T(8,128)}, f32[12,1024,256]{1,2,0:T(8,128)}) fusion(bf16[1024,12,64]{0,2,1:T(8,128)(2,1)} %bitcast.274, bf16[256,12,64]{0,2,1:T(8,128)(2,1)S(1)} %bitcast.266), kind=kOutput, calls=%fused_computation.212 | convolution fusion | flops 412090624 | bytes 14598144 | tf_op jit(solution)/shard_map/sub | solution.py:143
  86.2 5.8 %fusion.52 = bf16[12,64,1024]{2,1,0:T(8,128)(2,1)S(1)} fusion(bf16[256,12,64]{0,2,1:T(8,128)(2,1)S(1)} %bitcast.279, f32[12,1024,256]{1,2,0:T(8,128)} %get-tuple-element.52, f32[12,1024]{1,0:T(8,128)} %get-tuple-element.51), kind=kOutput, calls=%fused_computation.93 | convolution fusion | flops 409731072 | bytes 14598144 | tf_op jit(solution)/shard_map/htj,jhd->thd/dot_general | solution.py:147
  95.7 11.5 %fusion.15 = (bf16[3072,1024]{0,1:T(8,128)(2,1)}, f32[1024,3072]{1,0:T(8,128)}) fusion(f32[3072]{0:T(1024)S(1)} %copy-done.58, bf16[768,3072]{1,0:T(8,128)(2,1)S(1)} %bitcast.283, f32[1024,768]{1,0:T(8,128)S(1)} %get-tuple-element.54, f32[768]{0:T(1024)S(1)} %copy-done.34, f32[768]{0:T(1024)S(1)} %copy-done.32, f32[1024]{0:T(1024)S(1)} %add_rsqrt_fusion, ...), kind=kOutput, calls=%fused_computation.18 | convolution fusion | flops 4867227648 | bytes 26765312 | tf_op jit(solution)/shard_map/dot_general | solution.py:32
  109.7 16.2 %convert_reduce_fusion = (f32[3072]{0:T(1024)}, bf16[1024,3072]{1,0:T(8,128)(2,1)S(1)}) fusion(f32[1024,3072]{1,0:T(8,128)} %get-tuple-element.64, f32[3072]{0:T(1024)S(1)} %copy-done.59, bf16[1024,768]{1,0:T(8,128)(2,1)S(1)} %bitcast.256, bf16[3072,768]{1,0:T(8,128)(2,1)} %param.29), kind=kOutput, calls=%fused_computation.19 | convolution fusion | flops 4904186880 | bytes 25190400 | tf_op jit(solution)/shard_map/dot_general | solution.py:36
  125.9 8.7 %multiply_reduce_fusion.2 = (f32[768]{0:T(1024)}, f32[1024]{0:T(1024)S(1)}, f32[1024]{0:T(1024)S(1)}, f32[768]{0:T(1024)}, f32[1024,768]{1,0:T(8,128)S(1)}) fusion(f32[1024,768]{1,0:T(8,128)S(1)} %copy-done.3, f32[1024]{0:T(1024)S(1)} %add_rsqrt_fusion, f32[1024]{0:T(1024)S(1)} %broadcast_multiply_fusion.4, f32[768]{0:T(1024)S(1)} %copy-done.32, ...), kind=kOutput, calls=%fused_computation.62 | convolution fusion | flops 4838912000 | bytes 17327104 | tf_op jit(solution)/shard_map/dot_general | solution.py:36
  134.6 8.7 %fusion.99 = f32[768,3072]{1,0:T(8,128)} fusion(bf16[1024,3072]{1,0:T(8,128)(2,1)S(1)} %get-tuple-element.62, f32[1024,768]{1,0:T(8,128)S(1)} %copy-done.3, f32[768]{0:T(1024)S(1)} %copy-done.34, f32[768]{0:T(1024)S(1)} %copy-done.32, f32[1024]{0:T(1024)S(1)} %add_rsqrt_fusion, f32[1024]{0:T(1024)S(1)} %broadcast_multiply_fusion.4), kind=kOutput, calls=%fused_computation.209 | convolution fusion | flops 4835770368 | bytes 18888704 | tf_op jit(solution)/shard_map/dot_general | solution.py:40
  152.1 5.6 %multiply_reduce_fusion = (f32[12,1024]{1,0:T(8,128)S(1)}, f32[12,1024,256]{1,2,0:T(8,128)}) fusion(f32[12,1024,256]{1,2,0:T(8,128)S(1)} %bitcast.248, f32[12,1024]{1,0:T(8,128)S(1)} %copy-done.31, bf16[1024,12,64]{0,2,1:T(8,128)(2,1)S(1)} %bitcast.287, bf16[256,12,64]{0,2,1:T(8,128)(2,1)S(1)} %bitcast.280), kind=kOutput, calls=%fused_computation.21 | convolution fusion | flops 412078080 | bytes 27230208 | tf_op jit(solution)/shard_map/thd,jhd->htj/dot_general | solution.py:175
  157.8 7.0 %multiply_convert_fusion = bf16[12,1024,256]{1,2,0:T(8,128)(2,1)S(1)} fusion(f32[12,1024,256]{1,2,0:T(8,128)} %get-tuple-element.57, f32[12,1024]{1,0:T(8,128)S(1)} %get-tuple-element.56, f32[12,1024,256]{1,2,0:T(8,128)S(1)} %bitcast.248, f32[12,1024]{1,0:T(8,128)S(1)} %copy-done.31), kind=kLoop, calls=%fused_computation.20 | loop fusion | flops 12582912 | bytes 31555584 | tf_op jit(solution)/shard_map/convert_element_type | solution.py:177
  179.8 8.6 %copy.73 = bf16[3072,1024]{1,0:T(8,128)(2,1)} copy(bf16[3072,1024]{0,1:T(8,128)(2,1)} %get-tuple-element.63) | data formatting | bytes 12582912 | tf_op jit(solution)/shard_map/convert_element_type | solution.py:156
  188.5 13.4 %select_convert_fusion = bf16[1024,768]{1,0:T(8,128)(2,1)} fusion(f32[1024,768]{1,0:T(8,128)} %copy-done.2, bf16[3072,768]{1,0:T(8,128)(2,1)} %param.29, f32[1024,3072]{1,0:T(8,128)} %get-tuple-element.64, f32[3072]{0:T(1024)S(1)} %copy-done.60, f32[768]{0:T(1024)S(1)} %copy-done.62, pred[]{:T(512)S(6)} %lt.150), kind=kOutput, calls=%fused_computation.68 | convolution fusion | flops 4866441216 | bytes 22035456 | tf_op jit(solution)/shard_map/dot_general | solution.py:32
  201.9 4.7 all-to-all-start.1
  206.6 7.6 %fusion.105 = f32[8,2,192,768]{3,2,1,0:T(8,128)S(1)} fusion(bf16[8,2,192,1024]{3,2,1,0:T(8,128)(2,1)} %bitcast.255, bf16[1024,768,1,1]{1,0,3,2:T(8,128)(2,1)} %bitcast.257), kind=kOutput, calls=%fused_computation.215 | convolution fusion | flops 4831838208 | bytes 17301504 | tf_op jit(solution)/shard_map/dot_general | solution.py:40
  216.0 5.3 %collective-permute-start.18 = (bf16[8,192,768]{2,1,0:T(8,128)(2,1)}, bf16[8,192,768]{2,1,0:T(8,128)(2,1)}, u32[]{:S(2)}, u32[]{:S(2)}) collective-permute-start(bf16[8,192,768]{2,1,0:T(8,128)(2,1)} %fusion.46), channel_id=1, source_target_pairs={{0,8},{8,0},{16,24},{24,16},{1,9},{9,1},{17,25},{25,17},{2,10},{10... | collective-permute-start | bytes 7077896 | tf_op jit(solution)/shard_map/ppermute | solution.py:44
  262.5 41.7 %psum.7 = f32[8,1248]{1,0:T(8,128)S(1)} all-reduce(f32[8,1248]{1,0:T(8,128)S(1)} %concatenate.29), channel_id=1, replica_groups=mesh['batch'=4,'blk'=8] {'batch','blk'}, use_global_device_ids=true, to_apply=%region_21.22 | all-reduce | flops 9984 | bytes 79872 | tf_op jit(solution)/shard_map/psum | solution.py:241
  326.2 6.8 %collective-permute-start.11 = (f32[48,768]{1,0:T(8,128)S(1)}, f32[48,768]{1,0:T(8,128)S(1)}, u32[]{:S(2)}, u32[]{:S(2)}) collective-permute-start(f32[48,768]{1,0:T(8,128)S(1)} %convert_add_fusion.3), channel_id=1, source_target_pairs={{0,8},{8,0},{16,24},{24,16},{1,9},{9,1},{17,25},{25,17},{2,10},{10... | collective-permute-start | bytes 442376 | tf_op jit(solution)/shard_map/ppermute | solution.py:44
  348.4 23.6 %collective-permute-done.1 = bf16[4,1,48,2304]{3,2,0,1:T(8,128)(2,1)} collective-permute-done((bf16[4,1,48,2304]{3,2,0,1:T(8,128)(2,1)}, bf16[4,1,48,2304]{3,2,0,1:T(8,128)(2,1)}, u32[]{:S(2)}, u32[]{:S(2)}) %collective-permute-start.1) | collective-permute-done | bytes 884768 | tf_op jit(solution)/shard_map/ppermute | solution.py:44
  382.1 7.9 %collective-permute-done.2 = bf16[2,1,48,2304]{3,2,0,1:T(8,128)(2,1)S(1)} collective-permute-done((bf16[2,1,48,2304]{3,2,0,1:T(8,128)(2,1)}, bf16[2,1,48,2304]{3,2,0,1:T(8,128)(2,1)S(1)}, u32[]{:S(2)}, u32[]{:S(2)}) %collective-permute-start.2) | collective-permute-done | bytes 442400 | tf_op jit(solution)/shard_map/ppermute | solution.py:44
  391.4 10.1 %collective-permute-done.19 = bf16[4,1,192,768]{3,2,0,1:T(8,128)(2,1)} collective-permute-done((bf16[4,1,192,768]{3,2,0,1:T(8,128)(2,1)S(1)}, bf16[4,1,192,768]{3,2,0,1:T(8,128)(2,1)}, u32[]{:S(2)}, u32[]{:S(2)}) %collective-permute-start.19) | collective-permute-done | bytes 1179680 | tf_op jit(solution)/shard_map/ppermute | solution.py:44
  404.4 22.3 %collective-permute-done.13 = bf16[4,1,48,3072]{3,2,0,1:T(8,128)(2,1)} collective-permute-done((bf16[4,1,48,3072]{3,2,0,1:T(8,128)(2,1)}, bf16[4,1,48,3072]{3,2,0,1:T(8,128)(2,1)}, u32[]{:S(2)}, u32[]{:S(2)}) %collective-permute-start.13) | collective-permute-done | bytes 1179680 | tf_op jit(solution)/shard_map/ppermute | solution.py:44
  430.8 18.0 %collective-permute-done.14 = bf16[2,1,48,3072]{3,2,0,1:T(8,128)(2,1)S(1)} collective-permute-done((bf16[2,1,48,3072]{3,2,0,1:T(8,128)(2,1)S(1)}, bf16[2,1,48,3072]{3,2,0,1:T(8,128)(2,1)S(1)}, u32[]{:S(2)}, u32[]{:S(2)}) %collective-permute-start.14) | collective-permute-done | bytes 589856 | tf_op jit(solution)/shard_map/ppermute | solution.py:44
  452.1 12.1 %collective-permute-done.15 = bf16[1,1,48,3072]{3,2,0,1:T(8,128)(2,1)S(1)} collective-permute-done((bf16[1,1,48,3072]{3,2,0,1:T(8,128)(2,1)S(1)}, bf16[1,1,48,3072]{3,2,0,1:T(8,128)(2,1)S(1)}, u32[]{:S(2)}, u32[]{:S(2)}) %collective-permute-start.15) | collective-permute-done | bytes 294944 | tf_op jit(solution)/shard_map/ppermute | solution.py:44
  466.6 5.8 %collective-permute-done.16 = bf16[48,3072]{1,0:T(8,128)(2,1)S(1)} collective-permute-done((bf16[48,3072]{1,0:T(8,128)(2,1)S(1)}, bf16[48,3072]{1,0:T(8,128)(2,1)S(1)}, u32[]{:S(2)}, u32[]{:S(2)}) %collective-permute-start.16) | collective-permute-done | bytes 294944 | tf_op jit(solution)/shard_map/ppermute | solution.py:44
  (330 shorter events, 157.3 us)
Async XLA Ops:
  0.7 60.5 %all-to-all-start = ((bf16[8,128,768]{2,1,0:T(8,128)(2,1)}), bf16[8,128,768]{2,1,0:T(8,128)(2,1)S(1)}, u32[]{:S(2)}, u32[]{:S(2)}) async-start(bf16[8,128,768]{2,1,0:T(8,128)(2,1)} %param.16), calls=%async_computation | async-start | bytes 3145728 | tf_op jit(solution)/shard_map/all_to_all | solution.py:104
  61.2 46.0 %all-to-all-start.2 = ((bf16[8,128,768]{2,1,0:T(8,128)(2,1)}), bf16[8,128,768]{2,1,0:T(8,128)(2,1)}, u32[]{:S(2)}, u32[]{:S(2)}) async-start(bf16[8,128,768]{2,1,0:T(8,128)(2,1)} %param.17), calls=%async_computation.2 | async-start | bytes 3145728 | tf_op jit(solution)/shard_map/all_to_all | solution.py:104
  201.9 137.2 %all-to-all-start.1 = ((bf16[8,128,768]{2,1,0:T(8,128)(2,1)}), bf16[8,128,768]{2,1,0:T(8,128)(2,1)}, u32[]{:S(2)}, u32[]{:S(2)}) async-start(bf16[8,128,768]{2,1,0:T(8,128)(2,1)} %bitcast.273), calls=%async_computation.1 | async-start | bytes 3145728 | tf_op jit(solution)/shard_map/all_to_all | solution.py:109
  216.0 126.9 %collective-permute-start.18 = (bf16[8,192,768]{2,1,0:T(8,128)(2,1)}, bf16[8,192,768]{2,1,0:T(8,128)(2,1)}, u32[]{:S(2)}, u32[]{:S(2)}) collective-permute-start(bf16[8,192,768]{2,1,0:T(8,128)(2,1)} %fusion.46), channel_id=1, source_target_pairs={{0,8},{8,0},{16,24},{24,16},{1,9},{9,1},{17,25},{25,17},{2,10},{10... | collective-permute-start | bytes 7077896 | tf_op jit(solution)/shard_map/ppermute | solution.py:44
  224.1 81.4 %collective-permute-start.6 = (bf16[8,48,768]{2,1,0:T(8,128)(2,1)S(1)}, bf16[8,48,768]{2,1,0:T(8,128)(2,1)}, u32[]{:S(2)}, u32[]{:S(2)}) collective-permute-start(bf16[8,48,768]{2,1,0:T(8,128)(2,1)S(1)} %fusion.70), channel_id=1, source_target_pairs={{0,8},{8,0},{16,24},{24,16},{1,9},{9,1},{17,25},{25,17},{2,10},{10... | collective-permute-start | bytes 1769480 | tf_op jit(solution)/shard_map/ppermute | solution.py:44
  232.4 142.3 %collective-permute-start.12 = (bf16[8,48,3072]{2,1,0:T(8,128)(2,1)}, bf16[8,48,3072]{2,1,0:T(8,128)(2,1)}, u32[]{:S(2)}, u32[]{:S(2)}) collective-permute-start(bf16[8,48,3072]{2,1,0:T(8,128)(2,1)} %fusion.47), channel_id=1, source_target_pairs={{0,8},{8,0},{16,24},{24,16},{1,9},{9,1},{17,25},{25,17},{2,10},{10... | collective-permute-start | bytes 7077896 | tf_op jit(solution)/shard_map/ppermute | solution.py:44
  241.4 12.5 %collective-permute-start.24 = (bf16[8,128,128]{2,1,0:T(8,128)(2,1)}, bf16[8,128,128]{2,1,0:T(8,128)(2,1)}, u32[]{:S(2)}, u32[]{:S(2)}) collective-permute-start(bf16[8,128,128]{2,1,0:T(8,128)(2,1)} %bitcast.281), channel_id=1, source_target_pairs={{0,8},{8,0},{16,24},{24,16},{1,9},{9,1},{17,25},{25,17},{2,10},{10... | collective-permute-start | bytes 786440 | tf_op jit(solution)/shard_map/ppermute | solution.py:44
  258.2 74.8 %collective-permute-start = (bf16[8,48,2304]{2,1,0:T(8,128)(2,1)}, bf16[8,48,2304]{2,1,0:T(8,128)(2,1)}, u32[]{:S(2)}, u32[]{:S(2)}) collective-permute-start(bf16[8,48,2304]{2,1,0:T(8,128)(2,1)} %fusion.51), channel_id=1, source_target_pairs={{0,8},{8,0},{16,24},{24,16},{1,9},{9,1},{17,25},{25,17},{2,10},{10... | collective-permute-start | bytes 5308424 | tf_op jit(solution)/shard_map/ppermute | solution.py:44
  260.6 43.7 %collective-permute-start.26 = (bf16[2,1,128,128]{3,2,0,1:T(8,128)(2,1)S(1)}, bf16[2,1,128,128]{3,2,0,1:T(8,128)(2,1)S(1)}, u32[]{:S(2)}, u32[]{:S(2)}) collective-permute-start(bf16[2,1,128,128]{3,2,0,1:T(8,128)(2,1)S(1)} %fusion.85), channel_id=1, source_target_pairs={{0,2},{1,3},{2,0},{3,1},{4,6},{5,7},{6,4},{7,5},{8,10},{9,11},{10,... | collective-permute-start | bytes 196616 | tf_op jit(solution)/shard_map/ppermute | solution.py:44
  326.2 12.1 %collective-permute-start.11 = (f32[48,768]{1,0:T(8,128)S(1)}, f32[48,768]{1,0:T(8,128)S(1)}, u32[]{:S(2)}, u32[]{:S(2)}) collective-permute-start(f32[48,768]{1,0:T(8,128)S(1)} %convert_add_fusion.3), channel_id=1, source_target_pairs={{0,8},{8,0},{16,24},{24,16},{1,9},{9,1},{17,25},{25,17},{2,10},{10... | collective-permute-start | bytes 442376 | tf_op jit(solution)/shard_map/ppermute | solution.py:44
  337.8 34.2 %collective-permute-start.1 = (bf16[4,1,48,2304]{3,2,0,1:T(8,128)(2,1)}, bf16[4,1,48,2304]{3,2,0,1:T(8,128)(2,1)}, u32[]{:S(2)}, u32[]{:S(2)}) collective-permute-start(bf16[4,1,48,2304]{3,2,0,1:T(8,128)(2,1)} %fusion.69), channel_id=1, source_target_pairs={{0,1},{1,0},{2,3},{3,2},{4,5},{5,4},{6,7},{7,6},{8,9},{9,8},{10,11... | collective-permute-start | bytes 2654216 | tf_op jit(solution)/shard_map/ppermute | solution.py:44
  339.1 43.0 %all-to-all-start.3 = ((bf16[8,128,768]{2,1,0:T(8,128)(2,1)}), bf16[8,128,768]{2,1,0:T(8,128)(2,1)S(1)}, u32[]{:S(2)}, u32[]{:S(2)}) async-start(bf16[8,128,768]{2,1,0:T(8,128)(2,1)} %bitcast.259), calls=%async_computation.3 | async-start | bytes 3145728 | tf_op jit(solution)/shard_map/all_to_all | solution.py:109
  346.9 54.5 %collective-permute-start.19 = (bf16[4,1,192,768]{3,2,0,1:T(8,128)(2,1)S(1)}, bf16[4,1,192,768]{3,2,0,1:T(8,128)(2,1)}, u32[]{:S(2)}, u32[]{:S(2)}) collective-permute-start(bf16[4,1,192,768]{3,2,0,1:T(8,128)(2,1)S(1)} %fusion.64), channel_id=1, source_target_pairs={{0,1},{1,0},{2,3},{3,2},{4,5},{5,4},{6,7},{7,6},{8,9},{9,8},{10,11... | collective-permute-start | bytes 3538952 | tf_op jit(solution)/shard_map/ppermute | solution.py:44
  374.2 15.7 %collective-permute-start.2 = (bf16[2,1,48,2304]{3,2,0,1:T(8,128)(2,1)}, bf16[2,1,48,2304]{3,2,0,1:T(8,128)(2,1)S(1)}, u32[]{:S(2)}, u32[]{:S(2)}) collective-permute-start(bf16[2,1,48,2304]{3,2,0,1:T(8,128)(2,1)} %fusion.73), channel_id=1, source_target_pairs={{0,2},{1,3},{2,0},{3,1},{4,6},{5,7},{6,4},{7,5},{8,10},{9,11},{10,... | collective-permute-start | bytes 1327112 | tf_op jit(solution)/shard_map/ppermute | solution.py:44
  380.7 46.0 %collective-permute-start.13 = (bf16[4,1,48,3072]{3,2,0,1:T(8,128)(2,1)}, bf16[4,1,48,3072]{3,2,0,1:T(8,128)(2,1)}, u32[]{:S(2)}, u32[]{:S(2)}) collective-permute-start(bf16[4,1,48,3072]{3,2,0,1:T(8,128)(2,1)} %fusion.63), channel_id=1, source_target_pairs={{0,1},{1,0},{2,3},{3,2},{4,5},{5,4},{6,7},{7,6},{8,9},{9,8},{10,11... | collective-permute-start | bytes 3538952 | tf_op jit(solution)/shard_map/ppermute | solution.py:44
  391.2 37.8 %collective-permute-start.3 = (bf16[1,1,48,2304]{3,2,0,1:T(8,128)(2,1)S(1)}, bf16[1,1,48,2304]{3,2,0,1:T(8,128)(2,1)S(1)}, u32[]{:S(2)}, u32[]{:S(2)}) collective-permute-start(bf16[1,1,48,2304]{3,2,0,1:T(8,128)(2,1)S(1)} %dynamic-slice_convert_fusion.9), channel_id=1, source_target_pairs={{0,4},{1,5},{2,6},{3,7},{4,0},{5,1},{6,2},{7,3},{8,12},{9,13},{10,... | collective-permute-start | bytes 663560 | tf_op jit(solution)/shard_map/ppermute | solution.py:44
  403.8 26.5 %collective-permute-start.20 = (bf16[2,1,192,768]{3,2,0,1:T(8,128)(2,1)S(1)}, bf16[2,1,192,768]{3,2,0,1:T(8,128)(2,1)S(1)}, u32[]{:S(2)}, u32[]{:S(2)}) collective-permute-start(bf16[2,1,192,768]{3,2,0,1:T(8,128)(2,1)S(1)} %fusion.72), channel_id=1, source_target_pairs={{0,2},{1,3},{2,0},{3,1},{4,6},{5,7},{6,4},{7,5},{8,10},{9,11},{10,... | collective-permute-start | bytes 1769480 | tf_op jit(solution)/shard_map/ppermute | solution.py:44
  428.4 20.4 %collective-permute-start.14 = (bf16[2,1,48,3072]{3,2,0,1:T(8,128)(2,1)S(1)}, bf16[2,1,48,3072]{3,2,0,1:T(8,128)(2,1)S(1)}, u32[]{:S(2)}, u32[]{:S(2)}) collective-permute-start(bf16[2,1,48,3072]{3,2,0,1:T(8,128)(2,1)S(1)} %fusion.71), channel_id=1, source_target_pairs={{0,2},{1,3},{2,0},{3,1},{4,6},{5,7},{6,4},{7,5},{8,10},{9,11},{10,... | collective-permute-start | bytes 1769480 | tf_op jit(solution)/shard_map/ppermute | solution.py:44
  429.0 20.0 %collective-permute-start.4 = (bf16[48,2304]{1,0:T(8,128)(2,1)S(1)}, bf16[48,2304]{1,0:T(8,128)(2,1)S(1)}, u32[]{:S(2)}, u32[]{:S(2)}) collective-permute-start(bf16[48,2304]{1,0:T(8,128)(2,1)S(1)} %fusion.78), channel_id=1, source_target_pairs={{0,16},{8,24},{16,0},{24,8},{1,17},{9,25},{17,1},{25,9},{2,18},{10... | collective-permute-start | bytes 663560 | tf_op jit(solution)/shard_map/ppermute | solution.py:44
  430.5 20.4 %collective-permute-start.21 = (bf16[1,1,192,768]{3,2,0,1:T(8,128)(2,1)S(1)}, bf16[1,1,192,768]{3,2,0,1:T(8,128)(2,1)S(1)}, u32[]{:S(2)}, u32[]{:S(2)}) collective-permute-start(bf16[1,1,192,768]{3,2,0,1:T(8,128)(2,1)S(1)} %dynamic-slice_convert_fusion.7), channel_id=1, source_target_pairs={{0,4},{1,5},{2,6},{3,7},{4,0},{5,1},{6,2},{7,3},{8,12},{9,13},{10,... | collective-permute-start | bytes 884744 | tf_op jit(solution)/shard_map/ppermute | solution.py:44
  449.0 15.2 %collective-permute-start.15 = (bf16[1,1,48,3072]{3,2,0,1:T(8,128)(2,1)S(1)}, bf16[1,1,48,3072]{3,2,0,1:T(8,128)(2,1)S(1)}, u32[]{:S(2)}, u32[]{:S(2)}) collective-permute-start(bf16[1,1,48,3072]{3,2,0,1:T(8,128)(2,1)S(1)} %dynamic-slice_convert_fusion.8), channel_id=1, source_target_pairs={{0,4},{1,5},{2,6},{3,7},{4,0},{5,1},{6,2},{7,3},{8,12},{9,13},{10,... | collective-permute-start | bytes 884744 | tf_op jit(solution)/shard_map/ppermute | solution.py:44
  449.1 16.4 %collective-permute-start.5 = (f32[48,2304]{1,0:T(8,128)S(1)}, f32[48,2304]{1,0:T(8,128)S(1)}, u32[]{:S(2)}, u32[]{:S(2)}) collective-permute-start(f32[48,2304]{1,0:T(8,128)S(1)} %convert_add_fusion.2), channel_id=1, source_target_pairs={{0,8},{8,0},{16,24},{24,16},{1,9},{9,1},{17,25},{25,17},{2,10},{10... | collective-permute-start | bytes 1327112 | tf_op jit(solution)/shard_map/ppermute | solution.py:44
  451.0 14.7 %collective-permute-start.22 = (bf16[192,768]{1,0:T(8,128)(2,1)S(1)}, bf16[192,768]{1,0:T(8,128)(2,1)S(1)}, u32[]{:S(2)}, u32[]{:S(2)}) collective-permute-start(bf16[192,768]{1,0:T(8,128)(2,1)S(1)} %fusion.76), channel_id=1, source_target_pairs={{0,16},{8,24},{16,0},{24,8},{1,17},{9,25},{17,1},{25,9},{2,18},{10... | collective-permute-start | bytes 884744 | tf_op jit(solution)/shard_map/ppermute | solution.py:44
  465.7 9.1 %collective-permute-start.23 = (f32[192,768]{1,0:T(8,128)S(1)}, f32[192,768]{1,0:T(8,128)S(1)}, u32[]{:S(2)}, u32[]{:S(2)}) collective-permute-start(f32[192,768]{1,0:T(8,128)S(1)} %convert_add_fusion), channel_id=1, source_target_pairs={{0,8},{8,0},{16,24},{24,16},{1,9},{9,1},{17,25},{25,17},{2,10},{10... | collective-permute-start | bytes 1769480 | tf_op jit(solution)/shard_map/ppermute | solution.py:44
  (87 other events, 794.0 us)
